TPU v7x, 256 devices: a whole 4x4x8 slice. The times are simulated.
256 devices in a mesh: comp: 4 (over y), gx: 16 (over z_hi, x), gy: 4 (over z_lo, core).
Axes of the slice: x: 4, y: 4, z: 8 (z_hi: 4, z_lo: 2; z = z_hi * 2 + z_lo), core: 2. Of those that a mesh axis runs over, the one named last changes fastest.
Arguments:
- state: float32 [32, 256, 128, 128], P('comp', 'gx', 'gy'), may hold values from -4 to 4
- levels: int32 [256, 128], P('gx', 'gy'), may hold values from 0 to 128
- reaction: float32 [3, 8, 8], replicated, may hold values from -2 to 2
Outputs:
- new_state: float32 [32, 256, 128, 128], P('comp', 'gx', 'gy')
Inputs may be any that keep to these rules, and one draw needn't show every extreme that they name: `levels`: 0 marks a land column, 128 a column of full depth.
All inputs are finite; a program needn't handle non-finite values.
Results may differ from a plain program's by a relative error of at most 0.00018.
Values sent between devices are 32-bit elements; how exact they have to be, the bound alone decides.
A program may use at most 64 MiB of HBM per device.

v0:
```python
import jax
import jax.numpy as jnp
from jax import lax
from jax.sharding import PartitionSpec as P

ITERS = 3
time_step = 0.25
lateral_mix = 0.05
vertical_mix = 0.1
pressure_scale = 0.05
thermal_coef = 1.0
haline_coef = 0.8
coriolis_mean = 0.5
coriolis_slope = 0.5


def padded_2(cells, sides, width):
    for axis, dim in sides:
        count = lax.axis_size(axis)
        head = lax.slice_in_dim(cells, 0, width, axis=dim)
        tail = lax.slice_in_dim(cells, cells.shape[dim] - width, cells.shape[dim], axis=dim)
        cells = jnp.concatenate(
            [
                lax.ppermute(tail, axis, [(i, (i + 1) % count) for i in range(count)]),
                cells,
                lax.ppermute(head, axis, [((i + 1) % count, i) for i in range(count)]),
            ],
            axis=dim,
        )
    return cells


def padded_to(lines, length):
    spare = -lines.shape[0] % length
    if not spare:
        return lines
    return jnp.concatenate([lines, jnp.zeros((spare, *lines.shape[1:]), lines.dtype)])


def from_root(value, axis, root):
    lines = jnp.where(lax.axis_index(axis) == root, value, jnp.zeros_like(value)).reshape(
        -1, *value.shape[1:][-1:]
    )
    padded = padded_to(lines, lax.axis_size(axis))
    own = lax.psum_scatter(padded, axis, scatter_dimension=0, tiled=True)
    return lax.all_gather(own, axis, axis=0, tiled=True)[: len(lines)].reshape(value.shape)


def along(padded, axis, shift):
    count_x = padded.shape[1] - 4
    count_y = padded.shape[2] - 4
    if axis == 1:
        return padded[:, 2 + shift : 2 + shift + count_x, 2 : 2 + count_y]
    return padded[:, 2 : 2 + count_x, 2 + shift : 2 + shift + count_y]


def centered(padded, axis):
    return (
        8.0 * (along(padded, axis, 1) - along(padded, axis, -1))
        - (along(padded, axis, 2) - along(padded, axis, -2))
    ) / 12.0


def smoothing(padded, axis):
    return (
        along(padded, axis, 2)
        + along(padded, axis, -2)
        - 4.0 * (along(padded, axis, 1) + along(padded, axis, -1))
        + 6.0 * along(padded, axis, 0)
    ) / 12.0


def transport(padded, east, north):
    return (
        east * centered(padded, 1)
        + jnp.abs(east) * smoothing(padded, 1)
        + north * centered(padded, 2)
        + jnp.abs(north) * smoothing(padded, 2)
    )


def lateral(padded):
    return (
        along(padded, 1, 1)
        + along(padded, 1, -1)
        + along(padded, 2, 1)
        + along(padded, 2, -1)
        - 4.0 * along(padded, 1, 0)
    )


def vertical(center):
    column = jnp.pad(center, ((0, 0), (0, 0), (0, 0), (1, 1)))
    return column[..., 2:] + column[..., :-2] - 2.0 * center


def dynamics_step(padded, mask, latitude, accumulate):
    center = padded[:, 2:-2, 2:-2]
    east = center[0]
    north = center[1]
    moving = padded[0:4]
    density = haline_coef * padded[3] - thermal_coef * padded[2]
    pressure = (pressure_scale * accumulate(density))[None]
    tendency = (
        lateral_mix * lateral(moving)
        + vertical_mix * vertical(center[0:4])
        - transport(moving, east, north)
    )
    rotation = (coriolis_mean + coriolis_slope * latitude)[None, :, None]
    push_east = tendency[0] + rotation * north - centered(pressure, 1)[0]
    push_north = tendency[1] - rotation * east - centered(pressure, 2)[0]
    tendency = jnp.stack([push_east, push_north, tendency[2], tendency[3]])
    advanced = center[0:4] + time_step * (1.5 * tendency - 0.5 * center[4:8])
    return jnp.concatenate([advanced * mask, tendency * mask])


def tracer_step(padded, velocity, mask, coupling):
    center = padded[:, 2:-2, 2:-2]
    growth = 2.0 * jax.nn.sigmoid(velocity[2])
    reacting = growth * jnp.einsum(
        "ij,jxyz->ixyz", coupling, center, precision=lax.Precision.HIGHEST
    )
    tendency = (
        lateral_mix * lateral(padded)
        + vertical_mix * vertical(center)
        + reacting
        - transport(padded, velocity[0], velocity[1])
    )
    return (center + time_step * tendency) * mask


def per_device(state, levels, reaction):
    cells_y = state.shape[2]
    depth_count = state.shape[3]
    slot = lax.axis_index("comp")
    row_first = lax.axis_index("gy") * cells_y
    total_rows = cells_y * lax.axis_size("gy")
    depth = lax.broadcasted_iota(jnp.int32, (1, 1, depth_count), 2)
    mask = (depth < levels[:, :, None]).astype(jnp.float32)
    lower = lax.broadcasted_iota(jnp.int32, (depth_count, depth_count), 0)
    higher = lax.broadcasted_iota(jnp.int32, (depth_count, depth_count), 1)
    summing = (lower <= higher).astype(jnp.float32)
    coupling = lax.dynamic_index_in_dim(reaction, jnp.maximum(slot - 1, 0), 0, keepdims=False)

    def accumulate(density):
        return jnp.dot(density, summing, precision=lax.Precision.HIGHEST)

    def global_rows(width):
        return row_first - width + lax.iota(jnp.int32, cells_y + 2 * width)

    def latitude(width):
        rows = global_rows(width)
        return 2.0 * rows.astype(jnp.float32) / float(total_rows - 1) - 1.0

    current = state * mask[None]
    for step in range(ITERS):
        extend_padded = padded_2(current, (("gx", 1), ("gy", 2)), 2)
        inside_rows = global_rows(2)
        region_latitude = latitude(0)

        def run_dynamics(operands):
            return dynamics_step(operands[0], operands[2], region_latitude, accumulate)

        def run_tracers(operands):
            return tracer_step(operands[0], operands[1], operands[2], coupling)

        current = lax.cond(
            slot == 0,
            run_dynamics,
            run_tracers,
            (
                extend_padded
                * ((inside_rows >= 0) & (inside_rows < total_rows)).astype(jnp.float32)[
                    None, None, :, None
                ],
                from_root(current[0:3], "comp", 0),
                mask,
            ),
        )
    return current


def solution(mesh):
    in_specs = (P("comp", "gx", "gy", None), P("gx", "gy"), P())
    out_specs = P("comp", "gx", "gy", None)
    return jax.shard_map(
        per_device, mesh=mesh, in_specs=in_specs, out_specs=out_specs, check_vma=False
    )
```

profile of v0, /device:TPU:78, one launch (start us, length us, event | category | flops | bytes accessed | tf_op | source)
XLA Modules:
  0.0 169.2 jit_solution(1472869630248358750)
XLA Ops:
  7.4 1.9 %broadcast_multiply_fusion = f32[8,16,32,128]{3,2,1,0:T(8,128)S(1)} fusion(f32[8,16,32,128]{3,2,1,0:T(8,128)} %param.9, f32[16,32,128]{2,1,0:T(8,128)S(1)} %fusion.99), kind=kLoop, calls=%fused_computation.174 | loop fusion | flops 524288 | bytes 4456448 | tf_op jit(solution)/shard_map/mul | solution.py:155
  10.5 4.5 %collective-permute-start = (f32[8,2,32,128]{3,2,1,0:T(8,128)S(1)}, f32[8,2,32,128]{3,2,1,0:T(8,128)S(1)}, u32[]{:S(2)}, u32[]{:S(2)}) collective-permute-start(f32[8,2,32,128]{3,2,1,0:T(8,128)S(1)} %get-tuple-element.152), channel_id=1, source_target_pairs={{0,4},{4,8},{8,12},{12,16},{16,20},{20,24},{24,28},{28,32},{32,36}... | collective-permute-start | bytes 786440 | tf_op jit(solution)/shard_map/ppermute | solution.py:24
  15.6 10.5 %collective-permute-done = f32[8,2,32,128]{3,2,1,0:T(8,128)S(1)} collective-permute-done((f32[8,2,32,128]{3,2,1,0:T(8,128)S(1)}, f32[8,2,32,128]{3,2,1,0:T(8,128)S(1)}, u32[]{:S(2)}, u32[]{:S(2)}) %collective-permute-start) | collective-permute-done | bytes 262176 | tf_op jit(solution)/shard_map/ppermute | solution.py:24
  26.1 6.5 %collective-permute-done.1 = f32[8,2,32,128]{3,2,1,0:T(8,128)S(1)} collective-permute-done((f32[8,2,32,128]{3,2,1,0:T(8,128)S(1)}, f32[8,2,32,128]{3,2,1,0:T(8,128)S(1)}, u32[]{:S(2)}, u32[]{:S(2)}) %collective-permute-start.1) | collective-permute-done | bytes 262176 | tf_op jit(solution)/shard_map/ppermute | solution.py:26
  35.2 3.3 %collective-permute-done.2 = f32[8,20,2,128]{3,2,1,0:T(2,128)S(1)} collective-permute-done((f32[8,20,2,128]{3,2,1,0:T(2,128)S(1)}, f32[8,20,2,128]{3,2,1,0:T(2,128)S(1)}, u32[]{:S(2)}, u32[]{:S(2)}) %collective-permute-start.2) | collective-permute-done | bytes 163872 | tf_op jit(solution)/shard_map/ppermute | solution.py:24
  39.1 2.3 %maximum_multiply_fusion = f32[8,20,36,128]{3,2,1,0:T(8,128)S(1)} fusion(f32[8,20,2,128]{3,2,1,0:T(2,128)} %collective-permute-done.3, f32[8,2,32,128]{3,2,1,0:T(8,128)} %copy-done.7, f32[8,16,32,128]{3,2,1,0:T(8,128)} %copy-done.2, f32[8,2,32,128]{3,2,1,0:T(8,128)} %copy-done.6, f32[8,20,2,128]{3,2,1,0:T(2,128)} %copy-done.8, f32[36]{0:T(128)S(1)} %and_convert_fusion), kind=kLoop, calls=%fused_computation.171 | loop fusion | flops 3686400 | bytes 5898384 | tf_op jit(solution)/shard_map/mul | solution.py:172
  41.4 14.7 %all_gather.9 = f32[1536,128]{1,0:T(8,128)S(1)} all-gather(f32[384,128]{1,0:T(8,128)} %reduce-scatter.4.cloned.1.call-done), channel_id=1, replica_groups=mesh['comp'=4,'gx'=16,'gy'=4] {'comp'}, dimensions={0}, use_global_device_ids=true | all-gather | bytes 983040 | tf_op jit(solution)/shard_map/all_gather | solution.py:46
  56.1 8.6 %conditional.3 = (f32[8,16,32,128]{3,2,1,0:T(8,128)S(1)}) conditional(s32[]{:T(128)} %convert_element_type.41, (f32[8,20,36,128]{3,2,1,0:T(8,128)S(1)}, f32[1536,128]{1,0:T(8,128)S(1)}, f32[8,8]{1,0:T(8,128)S(1)}, f32[16,32,128]{2,1,0:T(8,128)S(1)}) %tuple.23, (f32[8,20,36,128]{3,2,1,0:T(8,128)S(1)}, f32[32]{0:T(128)S(1)}, f32[128,128]{1,0:T(8,128)}, ...), branch_computations={%region_1.2_spmd, %region_2.3_spmd} | conditional | flops 155859008 | bytes 41029640 | solution.py:167
  58.1 6.1 %fusion.8 = f32[8,16,32,128]{3,0,2,1:T(8,128)S(1)} fusion(f32[8,16,32,128]{3,0,2,1:T(8,128)S(1)} %slice.582, f32[8,20,36,128]{3,0,2,1:T(8,128)S(1)} %copy.9, f32[16,32,128]{2,1,0:T(8,128)S(1)} %get-tuple-element.68, f32[16,32,128]{2,1,0:T(8,128)S(1)} %bitcast.91, f32[16,32,128]{2,1,0:T(8,128)S(1)} %bitcast.93, f32[16,32,128]{2,1,0:T(8,128)S(1)} %bitcast.90, ...), kind=kOutput, calls=%fused_computation.10 | convolution fusion | flops 72351744 | bytes 24645632 | tf_op jit(solution)/shard_map/cond/branch_0_fun/ij,jxyz->ixyz/dot_general | solution.py:120
  68.0 6.3 %collective-permute-done.4 = f32[8,2,32,128]{3,2,1,0:T(8,128)S(1)} collective-permute-done((f32[8,2,32,128]{3,2,1,0:T(8,128)S(1)}, f32[8,2,32,128]{3,2,1,0:T(8,128)S(1)}, u32[]{:S(2)}, u32[]{:S(2)}) %collective-permute-start.4) | collective-permute-done | bytes 262176 | tf_op jit(solution)/shard_map/ppermute | solution.py:24
  74.3 6.8 %collective-permute-done.5 = f32[8,2,32,128]{3,2,1,0:T(8,128)S(1)} collective-permute-done((f32[8,2,32,128]{3,2,1,0:T(8,128)S(1)}, f32[8,2,32,128]{3,2,1,0:T(8,128)S(1)}, u32[]{:S(2)}, u32[]{:S(2)}) %collective-permute-start.5) | collective-permute-done | bytes 262176 | tf_op jit(solution)/shard_map/ppermute | solution.py:26
  83.1 4.7 %collective-permute-done.6 = f32[8,20,2,128]{3,2,1,0:T(2,128)S(1)} collective-permute-done((f32[8,20,2,128]{3,2,1,0:T(2,128)S(1)}, f32[8,20,2,128]{3,2,1,0:T(2,128)S(1)}, u32[]{:S(2)}, u32[]{:S(2)}) %collective-permute-start.6) | collective-permute-done | bytes 163872 | tf_op jit(solution)/shard_map/ppermute | solution.py:24
  87.8 2.1 %maximum_multiply_fusion.1 = f32[8,20,36,128]{3,2,1,0:T(8,128)S(1)} fusion(f32[8,20,2,128]{3,2,1,0:T(2,128)S(1)} %collective-permute-done.7, f32[8,2,32,128]{3,2,1,0:T(8,128)S(1)} %collective-permute-done.5, f32[8,16,32,128]{3,2,1,0:T(8,128)} %copy-done.3, f32[8,2,32,128]{3,2,1,0:T(8,128)S(1)} %collective-permute-done.4, ...), kind=kLoop, calls=%fused_computation.172 | loop fusion | flops 3686400 | bytes 5898384 | tf_op jit(solution)/shard_map/mul | solution.py:172
  90.0 14.8 %all_gather.10 = f32[1536,128]{1,0:T(8,128)S(1)} all-gather(f32[384,128]{1,0:T(8,128)} %reduce-scatter.6.cloned.1.call-done), channel_id=1, replica_groups=mesh['comp'=4,'gx'=16,'gy'=4] {'comp'}, dimensions={0}, use_global_device_ids=true | all-gather | bytes 983040 | tf_op jit(solution)/shard_map/all_gather | solution.py:46
  104.8 8.6 %conditional.4 = (f32[8,16,32,128]{3,2,1,0:T(8,128)S(1)}) conditional(s32[]{:T(128)} %convert_element_type.41, (f32[8,20,36,128]{3,2,1,0:T(8,128)S(1)}, f32[1536,128]{1,0:T(8,128)S(1)}, f32[8,8]{1,0:T(8,128)S(1)}, f32[16,32,128]{2,1,0:T(8,128)S(1)}) %tuple.25, (f32[8,20,36,128]{3,2,1,0:T(8,128)S(1)}, f32[32]{0:T(128)S(1)}, f32[128,128]{1,0:T(8,128)}, ...), branch_computations={%region_4.5_spmd, %region_5.6_spmd} | conditional | flops 155859008 | bytes 41029640 | solution.py:167
  106.8 6.1 %fusion.41 = f32[8,16,32,128]{3,0,2,1:T(8,128)S(1)} fusion(f32[8,16,32,128]{3,0,2,1:T(8,128)S(1)} %slice.602, f32[8,20,36,128]{3,0,2,1:T(8,128)S(1)} %copy.10, f32[16,32,128]{2,1,0:T(8,128)S(1)} %get-tuple-element.76, f32[16,32,128]{2,1,0:T(8,128)S(1)} %bitcast.96, f32[16,32,128]{2,1,0:T(8,128)S(1)} %bitcast.98, f32[16,32,128]{2,1,0:T(8,128)S(1)} %bitcast.95, ...), kind=kOutput, calls=%fused_computation.67 | convolution fusion | flops 72351744 | bytes 24645632 | tf_op jit(solution)/shard_map/cond/branch_0_fun/ij,jxyz->ixyz/dot_general | solution.py:120
  114.6 2.0 %collective-permute-start.9 = (f32[8,2,32,128]{3,2,1,0:T(8,128)S(1)}, f32[8,2,32,128]{3,2,1,0:T(8,128)S(1)}, u32[]{:S(2)}, u32[]{:S(2)}) collective-permute-start(f32[8,2,32,128]{3,2,1,0:T(8,128)S(1)} %get-tuple-element.149), channel_id=1, source_target_pairs={{4,0},{8,4},{12,8},{16,12},{20,16},{24,20},{28,24},{32,28},{36,32}... | collective-permute-start | bytes 786440 | tf_op jit(solution)/shard_map/ppermute | solution.py:26
  116.6 6.1 %collective-permute-done.8 = f32[8,2,32,128]{3,2,1,0:T(8,128)S(1)} collective-permute-done((f32[8,2,32,128]{3,2,1,0:T(8,128)S(1)}, f32[8,2,32,128]{3,2,1,0:T(8,128)S(1)}, u32[]{:S(2)}, u32[]{:S(2)}) %collective-permute-start.8) | collective-permute-done | bytes 262176 | tf_op jit(solution)/shard_map/ppermute | solution.py:24
  122.7 6.2 %collective-permute-done.9 = f32[8,2,32,128]{3,2,1,0:T(8,128)S(1)} collective-permute-done((f32[8,2,32,128]{3,2,1,0:T(8,128)S(1)}, f32[8,2,32,128]{3,2,1,0:T(8,128)S(1)}, u32[]{:S(2)}, u32[]{:S(2)}) %collective-permute-start.9) | collective-permute-done | bytes 262176 | tf_op jit(solution)/shard_map/ppermute | solution.py:26
  130.9 3.0 %collective-permute-done.10 = f32[8,20,2,128]{3,2,1,0:T(2,128)S(1)} collective-permute-done((f32[8,20,2,128]{3,2,1,0:T(2,128)S(1)}, f32[8,20,2,128]{3,2,1,0:T(2,128)S(1)}, u32[]{:S(2)}, u32[]{:S(2)}) %collective-permute-start.10) | collective-permute-done | bytes 163872 | tf_op jit(solution)/shard_map/ppermute | solution.py:24
  135.3 2.1 %maximum_multiply_fusion.2 = f32[8,20,36,128]{3,2,1,0:T(8,128)S(1)} fusion(f32[8,20,2,128]{3,2,1,0:T(2,128)S(1)} %collective-permute-done.11, f32[8,2,32,128]{3,2,1,0:T(8,128)S(1)} %collective-permute-done.9, f32[8,16,32,128]{3,2,1,0:T(8,128)} %copy-done.4, f32[8,2,32,128]{3,2,1,0:T(8,128)S(1)} %collective-permute-done.8, ...), kind=kLoop, calls=%fused_computation.173 | loop fusion | flops 3686400 | bytes 5898384 | tf_op jit(solution)/shard_map/mul | solution.py:172
  137.5 14.5 %all_gather.11 = f32[1536,128]{1,0:T(8,128)S(1)} all-gather(f32[384,128]{1,0:T(8,128)} %reduce-scatter.8.cloned.1.call-done), channel_id=1, replica_groups=mesh['comp'=4,'gx'=16,'gy'=4] {'comp'}, dimensions={0}, use_global_device_ids=true | all-gather | bytes 983040 | tf_op jit(solution)/shard_map/all_gather | solution.py:46
  152.0 8.6 %conditional.5 = (f32[8,16,32,128]{3,2,1,0:T(8,128)S(1)}) conditional(s32[]{:T(128)} %convert_element_type.41, (f32[8,20,36,128]{3,2,1,0:T(8,128)S(1)}, f32[1536,128]{1,0:T(8,128)S(1)}, f32[8,8]{1,0:T(8,128)S(1)}, f32[16,32,128]{2,1,0:T(8,128)S(1)}) %tuple.27, (f32[8,20,36,128]{3,2,1,0:T(8,128)S(1)}, f32[32]{0:T(128)S(1)}, f32[128,128]{1,0:T(8,128)}, ...), branch_computations={%region_7.8_spmd, %region_8.9_spmd} | conditional | flops 155859008 | bytes 41029640 | solution.py:167
  154.0 6.1 %fusion.74 = f32[8,16,32,128]{3,0,2,1:T(8,128)S(1)} fusion(f32[8,16,32,128]{3,0,2,1:T(8,128)S(1)} %slice.622, f32[8,20,36,128]{3,0,2,1:T(8,128)S(1)} %copy.11, f32[16,32,128]{2,1,0:T(8,128)S(1)} %get-tuple-element.84, f32[16,32,128]{2,1,0:T(8,128)S(1)} %bitcast.101, f32[16,32,128]{2,1,0:T(8,128)S(1)} %bitcast.103, f32[16,32,128]{2,1,0:T(8,128)S(1)} %bitcast.100, ...), kind=kOutput, calls=%fused_computation.124 | convolution fusion | flops 72351744 | bytes 24645632 | tf_op jit(solution)/shard_map/cond/branch_0_fun/ij,jxyz->ixyz/dot_general | solution.py:120
  (68 shorter events, 25.0 us)
Async XLA Ops:
  6.5 9.1 %copy-start = (f32[3,8,8]{2,1,0:T(8,128)S(1)}, f32[3,8,8]{2,1,0:T(8,128)}, u32[]{:S(2)}) copy-start(f32[3,8,8]{2,1,0:T(8,128)} %param.11) | copy-start | bytes 2308
  6.5 34.9 %reduce-scatter.4.cloned.1.call-start = ((), (), s32[]{:S(2)}) async-start(), calls=%async_computation.3 | async-start | bytes 983040 | tf_op jit(solution)/shard_map/reduce_scatter | solution.py:45
  9.3 23.4 %copy-start.2 = (f32[8,16,32,128]{3,2,1,0:T(8,128)}, f32[8,16,32,128]{3,2,1,0:T(8,128)S(1)}, u32[]{:S(2)}) copy-start(f32[8,16,32,128]{3,2,1,0:T(8,128)S(1)} %broadcast_multiply_fusion) | copy-start | bytes 6291460
  10.4 79.5 %reduce-scatter.6.cloned.1.call-start = ((), (), s32[]{:S(2)}) async-start(), calls=%async_computation.4 | async-start | bytes 983040 | tf_op jit(solution)/shard_map/reduce_scatter | solution.py:45
  10.5 15.6 %collective-permute-start = (f32[8,2,32,128]{3,2,1,0:T(8,128)S(1)}, f32[8,2,32,128]{3,2,1,0:T(8,128)S(1)}, u32[]{:S(2)}, u32[]{:S(2)}) collective-permute-start(f32[8,2,32,128]{3,2,1,0:T(8,128)S(1)} %get-tuple-element.152), channel_id=1, source_target_pairs={{0,4},{4,8},{8,12},{12,16},{16,20},{20,24},{24,28},{28,32},{32,36}... | collective-permute-start | bytes 786440 | tf_op jit(solution)/shard_map/ppermute | solution.py:24
  15.0 17.6 %collective-permute-start.1 = (f32[8,2,32,128]{3,2,1,0:T(8,128)S(1)}, f32[8,2,32,128]{3,2,1,0:T(8,128)S(1)}, u32[]{:S(2)}, u32[]{:S(2)}) collective-permute-start(f32[8,2,32,128]{3,2,1,0:T(8,128)S(1)} %get-tuple-element.153), channel_id=1, source_target_pairs={{4,0},{8,4},{12,8},{16,12},{20,16},{24,20},{28,24},{32,28},{36,32}... | collective-permute-start | bytes 786440 | tf_op jit(solution)/shard_map/ppermute | solution.py:26
  26.1 12.4 %copy-start.6 = (f32[8,2,32,128]{3,2,1,0:T(8,128)}, f32[8,2,32,128]{3,2,1,0:T(8,128)S(1)}, u32[]{:S(2)}) copy-start(f32[8,2,32,128]{3,2,1,0:T(8,128)S(1)} %collective-permute-done) | copy-start | bytes 786436
  32.6 5.9 %copy-start.7 = (f32[8,2,32,128]{3,2,1,0:T(8,128)}, f32[8,2,32,128]{3,2,1,0:T(8,128)S(1)}, u32[]{:S(2)}) copy-start(f32[8,2,32,128]{3,2,1,0:T(8,128)S(1)} %collective-permute-done.1) | copy-start | bytes 786436
  32.7 5.7 %collective-permute-start.2 = (f32[8,20,2,128]{3,2,1,0:T(2,128)S(1)}, f32[8,20,2,128]{3,2,1,0:T(2,128)S(1)}, u32[]{:S(2)}, u32[]{:S(2)}) collective-permute-start(f32[8,20,2,128]{3,2,1,0:T(2,128)S(1)} %get-tuple-element.146), channel_id=1, source_target_pairs={{0,1},{1,2},{2,3},{3,0},{4,5},{5,6},{6,7},{7,4},{8,9},{9,10},{10,1... | collective-permute-start | bytes 491528 | tf_op jit(solution)/shard_map/ppermute | solution.py:24
  32.8 6.3 %collective-permute-start.3 = (f32[8,20,2,128]{3,2,1,0:T(2,128)S(1)}, f32[8,20,2,128]{3,2,1,0:T(2,128)}, u32[]{:S(2)}, u32[]{:S(2)}) collective-permute-start(f32[8,20,2,128]{3,2,1,0:T(2,128)S(1)} %get-tuple-element.147), channel_id=1, source_target_pairs={{1,0},{2,1},{3,2},{0,3},{5,4},{6,5},{7,6},{4,7},{9,8},{10,9},{11,1... | collective-permute-start | bytes 491528 | tf_op jit(solution)/shard_map/ppermute | solution.py:26
  35.2 20.9 %copy-start.9 = (f32[32]{0:T(128)S(1)}, f32[32]{0:T(128)}, u32[]{:S(2)}) copy-start(f32[32]{0:T(128)} %multiply_add_fusion.3) | copy-start | bytes 388
  64.7 16.6 %copy-start.3 = (f32[8,16,32,128]{3,2,1,0:T(8,128)}, f32[8,16,32,128]{3,2,1,0:T(8,128)S(1)}, u32[]{:S(2)}) copy-start(f32[8,16,32,128]{3,2,1,0:T(8,128)S(1)} %get-tuple-element.156) | copy-start | bytes 6291460
  65.8 71.6 %reduce-scatter.8.cloned.1.call-start = ((), (), s32[]{:S(2)}) async-start(), calls=%async_computation.5 | async-start | bytes 983040 | tf_op jit(solution)/shard_map/reduce_scatter | solution.py:45
  65.9 8.4 %collective-permute-start.4 = (f32[8,2,32,128]{3,2,1,0:T(8,128)S(1)}, f32[8,2,32,128]{3,2,1,0:T(8,128)S(1)}, u32[]{:S(2)}, u32[]{:S(2)}) collective-permute-start(f32[8,2,32,128]{3,2,1,0:T(8,128)S(1)} %get-tuple-element.150), channel_id=1, source_target_pairs={{0,4},{4,8},{8,12},{12,16},{16,20},{20,24},{24,28},{28,32},{32,36}... | collective-permute-start | bytes 786440 | tf_op jit(solution)/shard_map/ppermute | solution.py:24
  67.0 14.2 %collective-permute-start.5 = (f32[8,2,32,128]{3,2,1,0:T(8,128)S(1)}, f32[8,2,32,128]{3,2,1,0:T(8,128)S(1)}, u32[]{:S(2)}, u32[]{:S(2)}) collective-permute-start(f32[8,2,32,128]{3,2,1,0:T(8,128)S(1)} %get-tuple-element.151), channel_id=1, source_target_pairs={{4,0},{8,4},{12,8},{16,12},{20,16},{24,20},{28,24},{32,28},{36,32}... | collective-permute-start | bytes 786440 | tf_op jit(solution)/shard_map/ppermute | solution.py:26
  81.3 6.5 %collective-permute-start.6 = (f32[8,20,2,128]{3,2,1,0:T(2,128)S(1)}, f32[8,20,2,128]{3,2,1,0:T(2,128)S(1)}, u32[]{:S(2)}, u32[]{:S(2)}) collective-permute-start(f32[8,20,2,128]{3,2,1,0:T(2,128)S(1)} %get-tuple-element.144), channel_id=1, source_target_pairs={{0,1},{1,2},{2,3},{3,0},{4,5},{5,6},{6,7},{7,4},{8,9},{9,10},{10,1... | collective-permute-start | bytes 491528 | tf_op jit(solution)/shard_map/ppermute | solution.py:24
  81.4 6.4 %collective-permute-start.7 = (f32[8,20,2,128]{3,2,1,0:T(2,128)S(1)}, f32[8,20,2,128]{3,2,1,0:T(2,128)S(1)}, u32[]{:S(2)}, u32[]{:S(2)}) collective-permute-start(f32[8,20,2,128]{3,2,1,0:T(2,128)S(1)} %get-tuple-element.145), channel_id=1, source_target_pairs={{1,0},{2,1},{3,2},{0,3},{5,4},{6,5},{7,6},{4,7},{9,8},{10,9},{11,1... | collective-permute-start | bytes 491528 | tf_op jit(solution)/shard_map/ppermute | solution.py:26
  113.3 15.7 %copy-start.4 = (f32[8,16,32,128]{3,2,1,0:T(8,128)}, f32[8,16,32,128]{3,2,1,0:T(8,128)S(1)}, u32[]{:S(2)}) copy-start(f32[8,16,32,128]{3,2,1,0:T(8,128)S(1)} %get-tuple-element.157) | copy-start | bytes 6291460
  114.5 8.2 %collective-permute-start.8 = (f32[8,2,32,128]{3,2,1,0:T(8,128)S(1)}, f32[8,2,32,128]{3,2,1,0:T(8,128)S(1)}, u32[]{:S(2)}, u32[]{:S(2)}) collective-permute-start(f32[8,2,32,128]{3,2,1,0:T(8,128)S(1)} %get-tuple-element.148), channel_id=1, source_target_pairs={{0,4},{4,8},{8,12},{12,16},{16,20},{20,24},{24,28},{28,32},{32,36}... | collective-permute-start | bytes 786440 | tf_op jit(solution)/shard_map/ppermute | solution.py:24
  114.6 14.3 %collective-permute-start.9 = (f32[8,2,32,128]{3,2,1,0:T(8,128)S(1)}, f32[8,2,32,128]{3,2,1,0:T(8,128)S(1)}, u32[]{:S(2)}, u32[]{:S(2)}) collective-permute-start(f32[8,2,32,128]{3,2,1,0:T(8,128)S(1)} %get-tuple-element.149), channel_id=1, source_target_pairs={{4,0},{8,4},{12,8},{16,12},{20,16},{24,20},{28,24},{32,28},{36,32}... | collective-permute-start | bytes 786440 | tf_op jit(solution)/shard_map/ppermute | solution.py:26
  129.0 4.8 %collective-permute-start.10 = (f32[8,20,2,128]{3,2,1,0:T(2,128)S(1)}, f32[8,20,2,128]{3,2,1,0:T(2,128)S(1)}, u32[]{:S(2)}, u32[]{:S(2)}) collective-permute-start(f32[8,20,2,128]{3,2,1,0:T(2,128)S(1)} %get-tuple-element.142), channel_id=1, source_target_pairs={{0,1},{1,2},{2,3},{3,0},{4,5},{5,6},{6,7},{7,4},{8,9},{9,10},{10,1... | collective-permute-start | bytes 491528 | tf_op jit(solution)/shard_map/ppermute | solution.py:24
  129.1 6.2 %collective-permute-start.11 = (f32[8,20,2,128]{3,2,1,0:T(2,128)S(1)}, f32[8,20,2,128]{3,2,1,0:T(2,128)S(1)}, u32[]{:S(2)}, u32[]{:S(2)}) collective-permute-start(f32[8,20,2,128]{3,2,1,0:T(2,128)S(1)} %get-tuple-element.143), channel_id=1, source_target_pairs={{1,0},{2,1},{3,2},{0,3},{5,4},{6,5},{7,6},{4,7},{9,8},{10,9},{11,1... | collective-permute-start | bytes 491528 | tf_op jit(solution)/shard_map/ppermute | solution.py:26
  160.6 1.3 copy-start.5
  161.9 0.7 copy-start.1
  (1 other events, 0.7 us)
Sparse Core Ops, SparseCore 0:
  10.6 24.9 reduce-scatter.3
  65.9 20.7 reduce-scatter.5
  114.6 21.2 reduce-scatter.7
where the time goes:
time: 170 us; the launch traced here: 169 us
  waiting for transfers between devices  55 us (32%)
  blocking collectives  44 us (26%)
  matrix products  18.4 us (11%)
  other arithmetic  14.5 us (9%)
  starting transfers between devices  14.2 us (8%)
  between operations  13.3 us (8%)
  local copies, waits for them, and re-layouts  9.62 us (6%)
    all_gather x3, blocking collectives, from_root(): lax.all_gather(own, axis, axis=0, tiled=True)[:len(lines)]  44 us
    ppermute x6, waiting for transfers between devices, padded_2(): lax.ppermute(tail, axis, [(i, (i + 1) % count) for i in range(count)])  33.8 us
    ppermute x6, waiting for transfers between devices, padded_2(): lax.ppermute(head, axis, [((i + 1) % count, i) for i in range(count)])  21.1 us
    dot_general x3, matrix products, tracer_step(): jnp.einsum('ij,jxyz->ixyz', coupling, center, precision=lax.Precision.HIG...  18.4 us
    ppermute x6, starting transfers between devices, padded_2(): lax.ppermute(head, axis, [((i + 1) % count, i) for i in range(count)])  8.25 us
    mul x3, other arithmetic, per_device(): extend_padded * ((inside_rows >= 0) & (inside_rows < total_rows)).astype(...  6.49 us
    ppermute x6, starting transfers between devices, padded_2(): lax.ppermute(tail, axis, [(i, (i + 1) % count) for i in range(count)])  5.88 us
    another operation x3, local copies, waits for them, and re-layouts  5.13 us
  transfers between devices with their start and end apart: 15, of which 10 were waited for; matrix products, arithmetic and copies ran while one was open for 5% of the time, Pallas kernels for 0%

commit v1 on v0

--- a/solution.py
+++ b/solution.py
@@ -43,7 +43,9 @@
     )
     padded = padded_to(lines, lax.axis_size(axis))
     own = lax.psum_scatter(padded, axis, scatter_dimension=0, tiled=True)
-    return lax.all_gather(own, axis, axis=0, tiled=True)[: len(lines)].reshape(value.shape)
+    return jnp.concatenate(
+        lax.all_to_all(jnp.stack([own] * lax.axis_size(axis)), axis, 0, 0), axis=0
+    )[: len(lines)].reshape(value.shape)
 
 
 def along(padded, axis, shift):

time: 170 us -> 179 us (1.053)
  blocking collectives: 44 us -> 0 us
  starting transfers between devices: 14.2 us -> 38.2 us
  waiting for transfers between devices: 55 us -> 74.2 us
  local copies, waits for them, and re-layouts: 9.62 us -> 15.2 us
  other arithmetic: 14.5 us -> 18 us
    reduce_scatter x3, waiting for transfers between devices: 0.06 us -> 60.7 us  [from_root(): own = lax.psum_scatter(padded, axis, scatter_dimension=0, tiled=True)]
    all_gather x3 -> x0, blocking collectives: 44 us -> none  [from_root(): lax.all_gather(own, axis, axis=0, tiled=True)[:len(lines)]]
    ppermute x6, waiting for transfers between devices: 33.8 us -> 8.36 us  [padded_2(): lax.ppermute(tail, axis, [(i, (i + 1) % count) for i in range(count)])]
    all_to_all x0 -> x3, starting transfers between devices: none -> 20.9 us  [from_root(): lax.all_to_all(jnp.stack([own] * lax.axis_size(axis)), axis, 0, 0)]
    ppermute x6, waiting for transfers between devices: 21.1 us -> 1.82 us  [padded_2(): lax.ppermute(head, axis, [((i + 1) % count, i) for i in range(count)])]
    ppermute x6, starting transfers between devices: 5.88 us -> 12 us  [padded_2(): lax.ppermute(tail, axis, [(i, (i + 1) % count) for i in range(count)])]
    another operation x3 -> x6, local copies, waits for them, and re-layouts: 5.13 us -> 10.7 us  [the longest x3 5.58 us: from_root(): jnp.stack([own] * lax.axis_size(axis))]
    mul x3, other arithmetic: 0.44 us -> 3.86 us  [tracer_step(): growth * jnp.einsum('ij,jxyz->ixyz', coupling, center, precision=lax.Prec...]
  transfers between devices with their start and end apart: 15 -> 18, of which waited for: 10 -> 12; matrix products, arithmetic and copies ran while one was open for 5% -> 8% of each run, Pallas kernels for 0% -> 0%
where the time goes in v1:
time: 179 us; the launch traced here: 177 us
  waiting for transfers between devices  74.2 us (41%)
  starting transfers between devices  38.2 us (21%)
  matrix products  18.4 us (10%)
  other arithmetic  18 us (10%)
  local copies, waits for them, and re-layouts  15.2 us (8%)
  between operations  13.3 us (7%)
    reduce_scatter x3, waiting for transfers between devices, from_root(): own = lax.psum_scatter(padded, axis, scatter_dimension=0, tiled=True)  60.7 us
    all_to_all x3, starting transfers between devices, from_root(): lax.all_to_all(jnp.stack([own] * lax.axis_size(axis)), axis, 0, 0)  20.9 us
    dot_general x3, matrix products, tracer_step(): jnp.einsum('ij,jxyz->ixyz', coupling, center, precision=lax.Precision.HIG...  18.4 us
    ppermute x6, starting transfers between devices, padded_2(): lax.ppermute(tail, axis, [(i, (i + 1) % count) for i in range(count)])  12 us
    ppermute x6, waiting for transfers between devices, padded_2(): lax.ppermute(tail, axis, [(i, (i + 1) % count) for i in range(count)])  8.36 us
    mul x3, other arithmetic, per_device(): extend_padded * ((inside_rows >= 0) & (inside_rows < total_rows)).astype(...  6.64 us
    another operation x3, local copies, waits for them, and re-layouts, from_root(): jnp.stack([own] * lax.axis_size(axis))  5.58 us
    ppermute x6, starting transfers between devices, padded_2(): lax.ppermute(head, axis, [((i + 1) % count, i) for i in range(count)])  5.21 us
  transfers between devices with their start and end apart: 18, of which 12 were waited for; matrix products, arithmetic and copies ran while one was open for 8% of the time, Pallas kernels for 0%

profile of v1, /device:TPU:78, one launch (start us, length us, event | category | flops | bytes accessed | tf_op | source)
XLA Modules:
  0.0 177.4 jit_solution(18121609940832483084)
XLA Ops:
  7.4 1.9 %broadcast_multiply_fusion = f32[8,16,32,128]{3,2,1,0:T(8,128)S(1)} fusion(f32[8,16,32,128]{3,2,1,0:T(8,128)} %param.9, f32[16,32,128]{2,1,0:T(8,128)S(1)} %fusion.114), kind=kLoop, calls=%fused_computation.189 | loop fusion | flops 524288 | bytes 4456448 | tf_op jit(solution)/shard_map/mul | solution.py:157
  10.5 4.5 %collective-permute-start = (f32[8,2,32,128]{3,2,1,0:T(8,128)S(1)}, f32[8,2,32,128]{3,2,1,0:T(8,128)S(1)}, u32[]{:S(2)}, u32[]{:S(2)}) collective-permute-start(f32[8,2,32,128]{3,2,1,0:T(8,128)S(1)} %get-tuple-element.152), channel_id=1, source_target_pairs={{0,4},{4,8},{8,12},{12,16},{16,20},{20,24},{24,28},{28,32},{32,36}... | collective-permute-start | bytes 786440 | tf_op jit(solution)/shard_map/ppermute | solution.py:24
  15.5 20.0 %reduce-scatter.4.cloned.1.call-done = f32[384,128]{1,0:T(8,128)} async-done(((f32[1536,128]{1,0:T(8,128)}), f32[384,128]{1,0:T(8,128)}) %reduce-scatter.4.cloned.1.call-update) | async-done | bytes 196624 | tf_op jit(solution)/shard_map/reduce_scatter | solution.py:45
  35.5 1.8 %stack.18 = f32[4,384,128]{2,1,0:T(8,128)} broadcast(f32[384,128]{1,0:T(8,128)} %reduce-scatter.4.cloned.1.call-done), dimensions={1,2} | broadcast | bytes 983040 | tf_op jit(solution)/shard_map/stack | solution.py:47
  37.4 6.9 %all-to-all-start = ((f32[4,384,128]{2,1,0:T(8,128)}), f32[4,384,128]{2,1,0:T(8,128)}, u32[]{:S(2)}, u32[]{:S(2)}) async-start(f32[4,384,128]{2,1,0:T(8,128)} %stack.18), calls=%async_computation.1 | async-start | bytes 1572864 | tf_op jit(solution)/shard_map/all_to_all | solution.py:47
  47.0 2.4 %collective-permute-done.2 = f32[8,20,2,128]{3,2,1,0:T(2,128)S(1)} collective-permute-done((f32[8,20,2,128]{3,2,1,0:T(2,128)S(1)}, f32[8,20,2,128]{3,2,1,0:T(2,128)S(1)}, u32[]{:S(2)}, u32[]{:S(2)}) %collective-permute-start.2) | collective-permute-done | bytes 163872 | tf_op jit(solution)/shard_map/ppermute | solution.py:24
  50.1 2.3 %maximum_multiply_fusion = f32[8,20,36,128]{3,2,1,0:T(8,128)S(1)} fusion(f32[8,20,2,128]{3,2,1,0:T(2,128)} %collective-permute-done.3, f32[8,2,32,128]{3,2,1,0:T(8,128)} %copy-done.7, f32[8,16,32,128]{3,2,1,0:T(8,128)} %copy-done.2, f32[8,2,32,128]{3,2,1,0:T(8,128)} %copy-done.6, f32[8,20,2,128]{3,2,1,0:T(2,128)} %copy-done.12, f32[36]{0:T(128)S(1)} %and_convert_fusion), kind=kLoop, calls=%fused_computation.186 | loop fusion | flops 3686400 | bytes 5898384 | tf_op jit(solution)/shard_map/mul | solution.py:174
  53.7 9.7 %conditional.3 = (f32[8,16,32,128]{3,2,1,0:T(8,128)S(1)}) conditional(s32[]{:T(128)} %convert_element_type.41, (f32[8,20,36,128]{3,2,1,0:T(8,128)S(1)}, f32[4,384,128]{2,1,0:T(8,128)}, f32[8,8]{1,0:T(8,128)S(1)}, f32[16,32,128]{2,1,0:T(8,128)S(1)}) %tuple.23, (f32[8,20,36,128]{3,2,1,0:T(8,128)S(1)}, f32[32]{0:T(128)S(1)}, f32[128,128]{1,0:T(8,128)}, ...), branch_computations={%region_1.2_spmd, %region_2.3_spmd} | conditional | flops 155859008 | bytes 41029640 | solution.py:169
  56.8 6.1 %fusion.8 = f32[8,16,32,128]{3,0,2,1:T(8,128)S(1)} fusion(f32[8,16,32,128]{3,0,2,1:T(8,128)S(1)} %slice.573, f32[8,20,36,128]{3,0,2,1:T(8,128)S(1)} %copy.9, f32[16,32,128]{2,1,0:T(8,128)S(1)} %get-tuple-element.68, f32[16,32,128]{2,1,0:T(8,128)S(1)} %get-tuple-element.105, f32[16,32,128]{2,1,0:T(8,128)S(1)} %get-tuple-element.106, ...), kind=kOutput, calls=%fused_computation.10 | convolution fusion | flops 72351744 | bytes 24645632 | tf_op jit(solution)/shard_map/cond/branch_0_fun/ij,jxyz->ixyz/dot_general | solution.py:122
  64.5 3.5 %collective-permute-start.4 = (f32[8,2,32,128]{3,2,1,0:T(8,128)S(1)}, f32[8,2,32,128]{3,2,1,0:T(8,128)S(1)}, u32[]{:S(2)}, u32[]{:S(2)}) collective-permute-start(f32[8,2,32,128]{3,2,1,0:T(8,128)S(1)} %get-tuple-element.150), channel_id=1, source_target_pairs={{0,4},{4,8},{8,12},{12,16},{16,20},{20,24},{24,28},{28,32},{32,36}... | collective-permute-start | bytes 786440 | tf_op jit(solution)/shard_map/ppermute | solution.py:24
  68.1 20.4 %reduce-scatter.6.cloned.1.call-done = f32[384,128]{1,0:T(8,128)} async-done(((f32[1536,128]{1,0:T(8,128)}), f32[384,128]{1,0:T(8,128)}) %reduce-scatter.6.cloned.1.call-update) | async-done | bytes 196624 | tf_op jit(solution)/shard_map/reduce_scatter | solution.py:45
  88.5 1.9 %stack.22 = f32[4,384,128]{2,1,0:T(8,128)} broadcast(f32[384,128]{1,0:T(8,128)} %reduce-scatter.6.cloned.1.call-done), dimensions={1,2} | broadcast | bytes 983040 | tf_op jit(solution)/shard_map/stack | solution.py:47
  90.3 7.0 %all-to-all-start.1 = ((f32[4,384,128]{2,1,0:T(8,128)}), f32[4,384,128]{2,1,0:T(8,128)}, u32[]{:S(2)}, u32[]{:S(2)}) async-start(f32[4,384,128]{2,1,0:T(8,128)} %stack.22), calls=%async_computation.3 | async-start | bytes 1572864 | tf_op jit(solution)/shard_map/all_to_all | solution.py:47
  99.3 3.0 %collective-permute-done.6 = f32[8,20,2,128]{3,2,1,0:T(2,128)S(1)} collective-permute-done((f32[8,20,2,128]{3,2,1,0:T(2,128)S(1)}, f32[8,20,2,128]{3,2,1,0:T(2,128)S(1)}, u32[]{:S(2)}, u32[]{:S(2)}) %collective-permute-start.6) | collective-permute-done | bytes 163872 | tf_op jit(solution)/shard_map/ppermute | solution.py:24
  103.1 2.2 %maximum_multiply_fusion.1 = f32[8,20,36,128]{3,2,1,0:T(8,128)S(1)} fusion(f32[8,20,2,128]{3,2,1,0:T(2,128)S(1)} %collective-permute-done.7, f32[8,2,32,128]{3,2,1,0:T(8,128)} %copy-done.10, f32[8,16,32,128]{3,2,1,0:T(8,128)} %copy-done.3, f32[8,2,32,128]{3,2,1,0:T(8,128)} %copy-done.8, f32[8,20,2,128]{3,2,1,0:T(2,128)S(1)} %collective-permute-done.6, ...), kind=kLoop, calls=%fused_computation.187 | loop fusion | flops 3686400 | bytes 5898384 | tf_op jit(solution)/shard_map/mul | solution.py:174
  106.4 9.7 %conditional.4 = (f32[8,16,32,128]{3,2,1,0:T(8,128)S(1)}) conditional(s32[]{:T(128)} %convert_element_type.41, (f32[8,20,36,128]{3,2,1,0:T(8,128)S(1)}, f32[4,384,128]{2,1,0:T(8,128)}, f32[8,8]{1,0:T(8,128)S(1)}, f32[16,32,128]{2,1,0:T(8,128)S(1)}) %tuple.25, (f32[8,20,36,128]{3,2,1,0:T(8,128)S(1)}, f32[32]{0:T(128)S(1)}, f32[128,128]{1,0:T(8,128)}, ...), branch_computations={%region_4.5_spmd, %region_5.6_spmd} | conditional | flops 155859008 | bytes 41029640 | solution.py:169
  109.5 6.1 %fusion.46 = f32[8,16,32,128]{3,0,2,1:T(8,128)S(1)} fusion(f32[8,16,32,128]{3,0,2,1:T(8,128)S(1)} %slice.596, f32[8,20,36,128]{3,0,2,1:T(8,128)S(1)} %copy.10, f32[16,32,128]{2,1,0:T(8,128)S(1)} %get-tuple-element.76, f32[16,32,128]{2,1,0:T(8,128)S(1)} %get-tuple-element.118, f32[16,32,128]{2,1,0:T(8,128)S(1)} %get-tuple-element.119, ...), kind=kOutput, calls=%fused_computation.72 | convolution fusion | flops 72351744 | bytes 24645632 | tf_op jit(solution)/shard_map/cond/branch_0_fun/ij,jxyz->ixyz/dot_general | solution.py:122
  117.2 3.8 %collective-permute-start.8 = (f32[8,2,32,128]{3,2,1,0:T(8,128)S(1)}, f32[8,2,32,128]{3,2,1,0:T(8,128)S(1)}, u32[]{:S(2)}, u32[]{:S(2)}) collective-permute-start(f32[8,2,32,128]{3,2,1,0:T(8,128)S(1)} %get-tuple-element.148), channel_id=1, source_target_pairs={{0,4},{4,8},{8,12},{12,16},{16,20},{20,24},{24,28},{28,32},{32,36}... | collective-permute-start | bytes 786440 | tf_op jit(solution)/shard_map/ppermute | solution.py:24
  121.0 20.3 %reduce-scatter.8.cloned.1.call-done = f32[384,128]{1,0:T(8,128)} async-done(((f32[1536,128]{1,0:T(8,128)}), f32[384,128]{1,0:T(8,128)}) %reduce-scatter.8.cloned.1.call-update) | async-done | bytes 196624 | tf_op jit(solution)/shard_map/reduce_scatter | solution.py:45
  143.1 7.0 %all-to-all-start.2 = ((f32[4,384,128]{2,1,0:T(8,128)}), f32[4,384,128]{2,1,0:T(8,128)}, u32[]{:S(2)}, u32[]{:S(2)}) async-start(f32[4,384,128]{2,1,0:T(8,128)} %stack.23), calls=%async_computation.5 | async-start | bytes 1572864 | tf_op jit(solution)/shard_map/all_to_all | solution.py:47
  152.1 3.0 %collective-permute-done.10 = f32[8,20,2,128]{3,2,1,0:T(2,128)S(1)} collective-permute-done((f32[8,20,2,128]{3,2,1,0:T(2,128)S(1)}, f32[8,20,2,128]{3,2,1,0:T(2,128)S(1)}, u32[]{:S(2)}, u32[]{:S(2)}) %collective-permute-start.10) | collective-permute-done | bytes 163872 | tf_op jit(solution)/shard_map/ppermute | solution.py:24
  155.9 2.2 %maximum_multiply_fusion.2 = f32[8,20,36,128]{3,2,1,0:T(8,128)S(1)} fusion(f32[8,20,2,128]{3,2,1,0:T(2,128)S(1)} %collective-permute-done.11, f32[8,2,32,128]{3,2,1,0:T(8,128)} %copy-done.11, f32[8,16,32,128]{3,2,1,0:T(8,128)} %copy-done.4, f32[8,2,32,128]{3,2,1,0:T(8,128)} %copy-done.9, f32[8,20,2,128]{3,2,1,0:T(2,128)S(1)} %collective-permute-done.10, ...), kind=kLoop, calls=%fused_computation.188 | loop fusion | flops 3686400 | bytes 5898384 | tf_op jit(solution)/shard_map/mul | solution.py:174
  159.2 9.7 %conditional.5 = (f32[8,16,32,128]{3,2,1,0:T(8,128)S(1)}) conditional(s32[]{:T(128)} %convert_element_type.41, (f32[8,20,36,128]{3,2,1,0:T(8,128)S(1)}, f32[4,384,128]{2,1,0:T(8,128)}, f32[8,8]{1,0:T(8,128)S(1)}, f32[16,32,128]{2,1,0:T(8,128)S(1)}) %tuple.27, (f32[8,20,36,128]{3,2,1,0:T(8,128)S(1)}, f32[32]{0:T(128)S(1)}, f32[128,128]{1,0:T(8,128)}, ...), branch_computations={%region_7.8_spmd, %region_8.9_spmd} | conditional | flops 155859008 | bytes 41029640 | solution.py:169
  162.3 6.1 %fusion.84 = f32[8,16,32,128]{3,0,2,1:T(8,128)S(1)} fusion(f32[8,16,32,128]{3,0,2,1:T(8,128)S(1)} %slice.619, f32[8,20,36,128]{3,0,2,1:T(8,128)S(1)} %copy.11, f32[16,32,128]{2,1,0:T(8,128)S(1)} %get-tuple-element.84, f32[16,32,128]{2,1,0:T(8,128)S(1)} %get-tuple-element.131, f32[16,32,128]{2,1,0:T(8,128)S(1)} %get-tuple-element.132, ...), kind=kOutput, calls=%fused_computation.134 | convolution fusion | flops 72351744 | bytes 24645632 | tf_op jit(solution)/shard_map/cond/branch_0_fun/ij,jxyz->ixyz/dot_general | solution.py:122
  (82 shorter events, 31.6 us)
Async XLA Ops:
  6.5 9.0 %copy-start = (f32[3,8,8]{2,1,0:T(8,128)S(1)}, f32[3,8,8]{2,1,0:T(8,128)}, u32[]{:S(2)}) copy-start(f32[3,8,8]{2,1,0:T(8,128)} %param.11) | copy-start | bytes 2308
  6.5 29.0 %reduce-scatter.4.cloned.1.call-start = ((), (), s32[]{:S(2)}) async-start(), calls=%async_computation.6 | async-start | bytes 983040 | tf_op jit(solution)/shard_map/reduce_scatter | solution.py:45
  9.3 35.0 %copy-start.2 = (f32[8,16,32,128]{3,2,1,0:T(8,128)}, f32[8,16,32,128]{3,2,1,0:T(8,128)S(1)}, u32[]{:S(2)}) copy-start(f32[8,16,32,128]{3,2,1,0:T(8,128)S(1)} %broadcast_multiply_fusion) | copy-start | bytes 6291460
  10.5 33.9 %collective-permute-start = (f32[8,2,32,128]{3,2,1,0:T(8,128)S(1)}, f32[8,2,32,128]{3,2,1,0:T(8,128)S(1)}, u32[]{:S(2)}, u32[]{:S(2)}) collective-permute-start(f32[8,2,32,128]{3,2,1,0:T(8,128)S(1)} %get-tuple-element.152), channel_id=1, source_target_pairs={{0,4},{4,8},{8,12},{12,16},{16,20},{20,24},{24,28},{28,32},{32,36}... | collective-permute-start | bytes 786440 | tf_op jit(solution)/shard_map/ppermute | solution.py:24
  14.9 29.4 %collective-permute-start.1 = (f32[8,2,32,128]{3,2,1,0:T(8,128)S(1)}, f32[8,2,32,128]{3,2,1,0:T(8,128)S(1)}, u32[]{:S(2)}, u32[]{:S(2)}) collective-permute-start(f32[8,2,32,128]{3,2,1,0:T(8,128)S(1)} %get-tuple-element.153), channel_id=1, source_target_pairs={{4,0},{8,4},{12,8},{16,12},{20,16},{24,20},{28,24},{32,28},{36,32}... | collective-permute-start | bytes 786440 | tf_op jit(solution)/shard_map/ppermute | solution.py:26
  37.4 16.3 %all-to-all-start = ((f32[4,384,128]{2,1,0:T(8,128)}), f32[4,384,128]{2,1,0:T(8,128)}, u32[]{:S(2)}, u32[]{:S(2)}) async-start(f32[4,384,128]{2,1,0:T(8,128)} %stack.18), calls=%async_computation.1 | async-start | bytes 1572864 | tf_op jit(solution)/shard_map/all_to_all | solution.py:47
  44.3 44.1 %reduce-scatter.6.cloned.1.call-start = ((), (), s32[]{:S(2)}) async-start(), calls=%async_computation.7 | async-start | bytes 983040 | tf_op jit(solution)/shard_map/reduce_scatter | solution.py:45
  44.3 5.0 %copy-start.6 = (f32[8,2,32,128]{3,2,1,0:T(8,128)}, f32[8,2,32,128]{3,2,1,0:T(8,128)S(1)}, u32[]{:S(2)}) copy-start(f32[8,2,32,128]{3,2,1,0:T(8,128)S(1)} %collective-permute-done) | copy-start | bytes 786436
  44.5 4.8 %collective-permute-start.2 = (f32[8,20,2,128]{3,2,1,0:T(2,128)S(1)}, f32[8,20,2,128]{3,2,1,0:T(2,128)S(1)}, u32[]{:S(2)}, u32[]{:S(2)}) collective-permute-start(f32[8,20,2,128]{3,2,1,0:T(2,128)S(1)} %get-tuple-element.146), channel_id=1, source_target_pairs={{0,1},{1,2},{2,3},{3,0},{4,5},{5,6},{6,7},{7,4},{8,9},{9,10},{10,1... | collective-permute-start | bytes 491528 | tf_op jit(solution)/shard_map/ppermute | solution.py:24
  44.6 5.6 %collective-permute-start.3 = (f32[8,20,2,128]{3,2,1,0:T(2,128)S(1)}, f32[8,20,2,128]{3,2,1,0:T(2,128)}, u32[]{:S(2)}, u32[]{:S(2)}) collective-permute-start(f32[8,20,2,128]{3,2,1,0:T(2,128)S(1)} %get-tuple-element.147), channel_id=1, source_target_pairs={{1,0},{2,1},{3,2},{0,3},{5,4},{6,5},{7,6},{4,7},{9,8},{10,9},{11,1... | collective-permute-start | bytes 491528 | tf_op jit(solution)/shard_map/ppermute | solution.py:26
  46.9 6.7 %copy-start.13 = (f32[32]{0:T(128)S(1)}, f32[32]{0:T(128)}, u32[]{:S(2)}) copy-start(f32[32]{0:T(128)} %multiply_add_fusion.3) | copy-start | bytes 388
  63.4 34.0 %copy-start.3 = (f32[8,16,32,128]{3,2,1,0:T(8,128)}, f32[8,16,32,128]{3,2,1,0:T(8,128)S(1)}, u32[]{:S(2)}) copy-start(f32[8,16,32,128]{3,2,1,0:T(8,128)S(1)} %get-tuple-element.156) | copy-start | bytes 6291460
  64.5 32.8 %collective-permute-start.4 = (f32[8,2,32,128]{3,2,1,0:T(8,128)S(1)}, f32[8,2,32,128]{3,2,1,0:T(8,128)S(1)}, u32[]{:S(2)}, u32[]{:S(2)}) collective-permute-start(f32[8,2,32,128]{3,2,1,0:T(8,128)S(1)} %get-tuple-element.150), channel_id=1, source_target_pairs={{0,4},{4,8},{8,12},{12,16},{16,20},{20,24},{24,28},{28,32},{32,36}... | collective-permute-start | bytes 786440 | tf_op jit(solution)/shard_map/ppermute | solution.py:24
  68.1 29.3 %collective-permute-start.5 = (f32[8,2,32,128]{3,2,1,0:T(8,128)S(1)}, f32[8,2,32,128]{3,2,1,0:T(8,128)S(1)}, u32[]{:S(2)}, u32[]{:S(2)}) collective-permute-start(f32[8,2,32,128]{3,2,1,0:T(8,128)S(1)} %get-tuple-element.151), channel_id=1, source_target_pairs={{4,0},{8,4},{12,8},{16,12},{20,16},{24,20},{28,24},{32,28},{36,32}... | collective-permute-start | bytes 786440 | tf_op jit(solution)/shard_map/ppermute | solution.py:26
  90.3 16.0 %all-to-all-start.1 = ((f32[4,384,128]{2,1,0:T(8,128)}), f32[4,384,128]{2,1,0:T(8,128)}, u32[]{:S(2)}, u32[]{:S(2)}) async-start(f32[4,384,128]{2,1,0:T(8,128)} %stack.22), calls=%async_computation.3 | async-start | bytes 1572864 | tf_op jit(solution)/shard_map/all_to_all | solution.py:47
  97.3 44.0 %reduce-scatter.8.cloned.1.call-start = ((), (), s32[]{:S(2)}) async-start(), calls=%async_computation.8 | async-start | bytes 983040 | tf_op jit(solution)/shard_map/reduce_scatter | solution.py:45
  97.5 4.8 %collective-permute-start.6 = (f32[8,20,2,128]{3,2,1,0:T(2,128)S(1)}, f32[8,20,2,128]{3,2,1,0:T(2,128)S(1)}, u32[]{:S(2)}, u32[]{:S(2)}) collective-permute-start(f32[8,20,2,128]{3,2,1,0:T(2,128)S(1)} %get-tuple-element.144), channel_id=1, source_target_pairs={{0,1},{1,2},{2,3},{3,0},{4,5},{5,6},{6,7},{7,4},{8,9},{9,10},{10,1... | collective-permute-start | bytes 491528 | tf_op jit(solution)/shard_map/ppermute | solution.py:24
  97.6 5.6 %collective-permute-start.7 = (f32[8,20,2,128]{3,2,1,0:T(2,128)S(1)}, f32[8,20,2,128]{3,2,1,0:T(2,128)S(1)}, u32[]{:S(2)}, u32[]{:S(2)}) collective-permute-start(f32[8,20,2,128]{3,2,1,0:T(2,128)S(1)} %get-tuple-element.145), channel_id=1, source_target_pairs={{1,0},{2,1},{3,2},{0,3},{5,4},{6,5},{7,6},{4,7},{9,8},{10,9},{11,1... | collective-permute-start | bytes 491528 | tf_op jit(solution)/shard_map/ppermute | solution.py:26
  116.1 34.0 %copy-start.4 = (f32[8,16,32,128]{3,2,1,0:T(8,128)}, f32[8,16,32,128]{3,2,1,0:T(8,128)S(1)}, u32[]{:S(2)}) copy-start(f32[8,16,32,128]{3,2,1,0:T(8,128)S(1)} %get-tuple-element.157) | copy-start | bytes 6291460
  117.2 32.9 %collective-permute-start.8 = (f32[8,2,32,128]{3,2,1,0:T(8,128)S(1)}, f32[8,2,32,128]{3,2,1,0:T(8,128)S(1)}, u32[]{:S(2)}, u32[]{:S(2)}) collective-permute-start(f32[8,2,32,128]{3,2,1,0:T(8,128)S(1)} %get-tuple-element.148), channel_id=1, source_target_pairs={{0,4},{4,8},{8,12},{12,16},{16,20},{20,24},{24,28},{28,32},{32,36}... | collective-permute-start | bytes 786440 | tf_op jit(solution)/shard_map/ppermute | solution.py:24
  121.0 29.1 %collective-permute-start.9 = (f32[8,2,32,128]{3,2,1,0:T(8,128)S(1)}, f32[8,2,32,128]{3,2,1,0:T(8,128)S(1)}, u32[]{:S(2)}, u32[]{:S(2)}) collective-permute-start(f32[8,2,32,128]{3,2,1,0:T(8,128)S(1)} %get-tuple-element.149), channel_id=1, source_target_pairs={{4,0},{8,4},{12,8},{16,12},{20,16},{24,20},{28,24},{32,28},{36,32}... | collective-permute-start | bytes 786440 | tf_op jit(solution)/shard_map/ppermute | solution.py:26
  143.1 16.0 %all-to-all-start.2 = ((f32[4,384,128]{2,1,0:T(8,128)}), f32[4,384,128]{2,1,0:T(8,128)}, u32[]{:S(2)}, u32[]{:S(2)}) async-start(f32[4,384,128]{2,1,0:T(8,128)} %stack.23), calls=%async_computation.5 | async-start | bytes 1572864 | tf_op jit(solution)/shard_map/all_to_all | solution.py:47
  150.3 4.8 %collective-permute-start.10 = (f32[8,20,2,128]{3,2,1,0:T(2,128)S(1)}, f32[8,20,2,128]{3,2,1,0:T(2,128)S(1)}, u32[]{:S(2)}, u32[]{:S(2)}) collective-permute-start(f32[8,20,2,128]{3,2,1,0:T(2,128)S(1)} %get-tuple-element.142), channel_id=1, source_target_pairs={{0,1},{1,2},{2,3},{3,0},{4,5},{5,6},{6,7},{7,4},{8,9},{9,10},{10,1... | collective-permute-start | bytes 491528 | tf_op jit(solution)/shard_map/ppermute | solution.py:24
  150.4 5.6 %collective-permute-start.11 = (f32[8,20,2,128]{3,2,1,0:T(2,128)S(1)}, f32[8,20,2,128]{3,2,1,0:T(2,128)S(1)}, u32[]{:S(2)}, u32[]{:S(2)}) collective-permute-start(f32[8,20,2,128]{3,2,1,0:T(2,128)S(1)} %get-tuple-element.143), channel_id=1, source_target_pairs={{1,0},{2,1},{3,2},{0,3},{5,4},{6,5},{7,6},{4,7},{9,8},{10,9},{11,1... | collective-permute-start | bytes 491528 | tf_op jit(solution)/shard_map/ppermute | solution.py:26
  (8 other events, 27.5 us)
Sparse Core Ops, SparseCore 0:
  10.5 24.9 reduce-scatter.3
  64.6 23.8 reduce-scatter.5
  117.3 23.9 reduce-scatter.7
